TPU v7x, 32 devices: a whole 2x2x4 slice. The times are simulated.
32 devices in a mesh: grp: 2 (over y), row: 8 (over z, x), col: 2 (over core).
Axes of the slice: x: 2, y: 2, z: 4, core: 2. Of those that a mesh axis runs over, the one named last changes fastest.
Arguments:
- grad_out: bfloat16 [1024, 8192], P(('grp', 'row'), 'col'), parts along dimension 0, may hold values from -6 to 6
- hidden_act: bfloat16 [1024, 22016], P(('grp', 'col'), 'row'), parts along dimension 0, may hold values from -6 to 6
- down_weight: bfloat16 [22016, 8192], P('row', 'col'), may hold values from -0.0390625 to 0.0390625
- proj_in: bfloat16 [22016, 64], P('row'), may hold values from -0.0390625 to 0.0390625
- proj_out: bfloat16 [8192, 64], P('col'), may hold values from -0.0625 to 0.0625
- queries: bfloat16 [128, 4096], P('row', 'col'), may hold values from -0.01171875 to 0.01171875
- example_ids: int32 [1024], P(('grp', 'row')), parts along dimension 0, may hold values from 0 to 7, never falling along the last dimension, each value on 1 to 128 neighbouring positions
Outputs:
- grad_hidden: bfloat16 [1024, 22016], P(('grp', 'col'), 'row'), parts along dimension 0
- weight_grad: bfloat16 [44032, 8192], P(('grp', 'row'), 'col'), parts along dimension 0
- scores: float32 [128, 16], P(('row', 'col'), 'grp'), parts along dimension 1
There are 2 independent parts, one for each index of `grp`. A program takes and returns all parts, laid end to end along the dimension named above; an argument that names none is the same for every part. Nothing has to cross between parts.
Inputs may be any that keep to these rules, and one draw needn't show every extreme that they name: `example_ids`: never falling along the tokens; each example holds 1 to 128 tokens, one exactly 128.
All inputs are finite; a program needn't handle non-finite values.
Results may differ from a plain program's by a relative error of at most 0.001.
Values may be sent and summed in bfloat16 or wider, within the bound.
A program may use at most 192 MiB of HBM per device.

v0:
```python
import jax
import jax.numpy as jnp
from jax import lax
from jax.sharding import PartitionSpec as P

EXAMPLES = 8


def body(grad_out, hidden_act, down_weight, proj_in, proj_out, queries, example_ids):
    full_hidden = lax.all_gather(hidden_act, "col", axis=0, tiled=True)
    full_grad = lax.all_gather(grad_out, "row", axis=0, tiled=True)
    token_rows = full_grad
    grad_hidden = lax.psum_scatter(
        lax.dot_general(
            token_rows, down_weight, (((1,), (1,)), ((), ())), preferred_element_type=jnp.float32
        ),
        "col",
        scatter_dimension=0,
        tiled=True,
    ).astype(jnp.bfloat16)
    weight_grad = lax.dot_general(
        full_hidden, full_grad, (((0,), (0,)), ((), ())), preferred_element_type=jnp.float32
    ).astype(jnp.bfloat16)
    token_rows = full_hidden
    in_factor = lax.psum_scatter(
        jnp.dot(token_rows, proj_in, preferred_element_type=jnp.float32),
        "row",
        scatter_dimension=0,
        tiled=True,
    )
    out_factor = lax.psum(jnp.dot(grad_out, proj_out, preferred_element_type=jnp.float32), "col")
    split_rank = in_factor.shape[1] // lax.axis_size("col")
    own_factor = lax.dynamic_slice_in_dim(
        in_factor, lax.axis_index("col") * split_rank, split_rank, 1
    )
    outer_terms = (own_factor[:, :, None] * out_factor[:, None, :]).reshape(own_factor.shape[0], -1)
    labels = jnp.arange(EXAMPLES, dtype=jnp.int32)
    onehot = (example_ids[None, :] == labels[:, None]).astype(jnp.float32)
    partial_grads = jnp.dot(onehot, outer_terms, precision=lax.Precision.HIGHEST)
    example_grads = lax.psum(partial_grads, "row")
    values = jnp.dot(queries.astype(jnp.float32), example_grads.T, precision=lax.Precision.HIGHEST)
    scores = lax.psum_scatter(values, "col", scatter_dimension=0, tiled=True)
    return (grad_hidden, weight_grad, scores)


def solution(mesh):
    return jax.shard_map(
        body,
        mesh=mesh,
        in_specs=(
            P(("grp", "row"), "col"),
            P(("grp", "col"), "row"),
            P("row", "col"),
            P("row", None),
            P("col", None),
            P("row", "col"),
            P(("grp", "row")),
        ),
        out_specs=(P(("grp", "col"), "row"), P(("grp", "row"), "col"), P(("row", "col"), "grp")),
        check_vma=False,
    )
```

profile of v0, /device:TPU:0, one launch (start us, length us, event | category | flops | bytes accessed | tf_op | source)
XLA Modules:
  0.0 267.6 jit_solution(11298728215527538428)
XLA Ops:
  7.2 0.0 copy-start
  7.2 0.0 copy-start.1
  7.2 0.0 all-gather.5.cloned.1.call-start
  7.2 0.7 all-gather.5.cloned.1.call-update
  7.9 0.0 copy-start.3
  7.9 0.0 reduce-scatter.6.cloned.1.call-start
  8.0 15.3 %all-gather.5.cloned.1.call-done = bf16[512,2752]{0,1:T(8,128)(2,1)} async-done(((bf16[256,2752]{0,1:T(8,128)(2,1)}), bf16[512,2752]{0,1:T(8,128)(2,1)}) %all-gather.5.cloned.1.call-update) | async-done | bytes 2818064 | tf_op jit(solution)/shard_map/all_gather | solution.py:10
  23.3 3.5 %fusion.3 = f32[512,64]{1,0:T(8,128)} fusion(bf16[512,2752]{0,1:T(8,128)(2,1)} %all-gather.5.cloned.1.call-done, bf16[2752,64]{0,1:T(8,128)(2,1)} %param.10), kind=kOutput, calls=%fused_computation.9 | convolution fusion | flops 180355072 | bytes 3301376 | tf_op jit(solution)/shard_map/dot_general | solution.py:26
  26.8 0.0 reduce-scatter.6.cloned.1.call-update
  26.8 0.0 all-gather.3.cloned.1.call-start
  26.9 0.7 all-gather.3.cloned.1.call-update
  27.6 0.0 all-reduce.3.cloned.1.call-start
  27.6 0.0 copy-done
  27.6 0.0 copy-done.1
  27.6 0.3 fusion.4
  27.9 3.5 %psum.14 = f32[64,64]{1,0:T(8,128)S(1)} all-reduce(f32[64,64]{1,0:T(8,128)S(1)} %fusion.4), channel_id=1, replica_groups=mesh['grp'=2,'row'=8,'col'=2] {'col'}, use_global_device_ids=true, to_apply=%region_2.0 | all-reduce | flops 4096 | bytes 32768 | tf_op jit(solution)/shard_map/psum | solution.py:31
  31.4 59.1 %reduce-scatter.6.cloned.1.call-done = f32[64,64]{1,0:T(8,128)} async-done(((f32[512,64]{1,0:T(8,128)}), f32[64,64]{1,0:T(8,128)}) %reduce-scatter.6.cloned.1.call-update) | async-done | bytes 16400 | tf_op jit(solution)/shard_map/reduce_scatter | solution.py:25
  90.5 0.8 constant_dynamic-slice_fusion.1
  91.3 0.3 broadcast_multiply_fusion
  91.7 0.4 mul.24
  92.1 0.0 copy-done.3
  92.1 0.9 fusion
  93.0 0.0 all-reduce.3.cloned.1.call-update
  93.0 0.0 reduce-scatter.4.cloned.1.call-start
  93.1 71.5 %all-gather.3.cloned.1.call-done = bf16[512,4096]{1,0:T(8,128)(2,1)} async-done(((bf16[64,4096]{1,0:T(8,128)(2,1)}), bf16[512,4096]{1,0:T(8,128)(2,1)}) %all-gather.3.cloned.1.call-update) | async-done | bytes 4194320 | tf_op jit(solution)/shard_map/all_gather | solution.py:11
  164.5 19.1 %fusion.2 = f32[512,2752]{0,1:T(8,128)} fusion(bf16[512,4096]{1,0:T(8,128)(2,1)} %all-gather.3.cloned.1.call-done, bf16[2752,4096]{1,0:T(8,128)(2,1)} %param.9), kind=kOutput, calls=%fused_computation.8 | convolution fusion | flops 11542724608 | bytes 32374784 | tf_op jit(solution)/shard_map/dot_general | solution.py:14
  183.6 0.0 copy-start.5
  183.6 0.0 copy-start.2
  183.6 0.0 copy-start.4
  183.6 0.0 reduce-scatter.4.cloned.1.call-update
  183.7 0.6 copy-done.5
  184.3 0.6 dynamic-slice
  185.5 50.7 %all-reduce.3.cloned.1.call-done = f32[8,2048]{1,0:T(8,128)} async-done(((f32[8,2048]{1,0:T(8,128)}), f32[8,2048]{1,0:T(8,128)}) %all-reduce.3.cloned.1.call-update) | async-done | bytes 65552 | tf_op jit(solution)/shard_map/psum | solution.py:40
  236.2 0.0 copy-done.2
  236.2 1.0 convolution_bitcast_fusion
  237.2 2.5 all-reduce
  239.7 0.1 constant_dynamic-slice_fusion
  239.8 0.7 copy.11
  240.5 0.0 copy-done.4
  240.5 17.6 %convolution_convert_fusion = bf16[2752,4096]{1,0:T(8,128)(2,1)} fusion(bf16[512,2752]{0,1:T(8,128)(2,1)S(1)} %copy-done.4, bf16[512,4096]{1,0:T(8,128)(2,1)} %all-gather.3.cloned.1.call-done), kind=kOutput, calls=%fused_computation | convolution fusion | flops 11553996800 | bytes 29556736 | tf_op jit(solution)/shard_map/dot_general | solution.py:21
  258.0 0.0 reduce-scatter.4.cloned.1.call-done
  258.0 3.0 %convert_element_type.8 = bf16[256,2752]{0,1:T(8,128)(2,1)} convert(f32[256,2752]{0,1:T(8,128)} %reduce-scatter.4.cloned.1.call-done) | non-fusion elementwise | flops 704512 | bytes 4227072 | tf_op jit(solution)/shard_map/convert_element_type | solution.py:20
Async XLA Ops:
  7.2 20.5 %copy-start = (bf16[4096,64]{0,1:T(8,128)(2,1)S(1)}, bf16[4096,64]{0,1:T(8,128)(2,1)}, u32[]{:S(2)}) copy-start(bf16[4096,64]{0,1:T(8,128)(2,1)} %param.11) | copy-start | bytes 1572868
  7.2 20.4 %copy-start.1 = (bf16[64,4096]{1,0:T(8,128)(2,1)S(1)}, bf16[64,4096]{1,0:T(8,128)(2,1)}, u32[]{:S(2)}) copy-start(bf16[64,4096]{1,0:T(8,128)(2,1)} %param.7) | copy-start | bytes 1572868
  7.2 16.1 %all-gather.5.cloned.1.call-start = ((), (), s32[]{:S(2)}) async-start(), calls=%async_computation.4 | async-start | bytes 4227072 | tf_op jit(solution)/shard_map/all_gather | solution.py:10
  7.9 84.1 %copy-start.3 = (s32[64]{0:T(128)S(1)}, s32[64]{0:T(128)}, u32[]{:S(2)}) copy-start(s32[64]{0:T(128)} %param.13) | copy-start | bytes 772
  7.9 82.6 %reduce-scatter.6.cloned.1.call-start = ((), (), s32[]{:S(2)}) async-start(), calls=%async_computation.5 | async-start | bytes 294912 | tf_op jit(solution)/shard_map/reduce_scatter | solution.py:25
  26.8 137.7 %all-gather.3.cloned.1.call-start = ((), (), s32[]{:S(2)}) async-start(), calls=%async_computation.2 | async-start | bytes 4718592 | tf_op jit(solution)/shard_map/all_gather | solution.py:11
  27.6 208.7 %all-reduce.3.cloned.1.call-start = ((), (), s32[]{:S(2)}) async-start(), calls=%async_computation.6 | async-start | bytes 131072 | tf_op jit(solution)/shard_map/psum | solution.py:40
  93.0 165.0 %reduce-scatter.4.cloned.1.call-start = ((), (), s32[]{:S(2)}) async-start(), calls=%async_computation.3 | async-start | bytes 8454144 | tf_op jit(solution)/shard_map/reduce_scatter | solution.py:13
  183.6 0.7 copy-start.5
  183.6 52.6 %copy-start.2 = (bf16[16,2048]{1,0:T(8,128)(2,1)S(1)}, bf16[16,2048]{1,0:T(8,128)(2,1)}, u32[]{:S(2)}) copy-start(bf16[16,2048]{1,0:T(8,128)(2,1)} %param.12) | copy-start | bytes 196612
  183.6 56.8 %copy-start.4 = (bf16[512,2752]{0,1:T(8,128)(2,1)S(1)}, bf16[512,2752]{0,1:T(8,128)(2,1)}, u32[]{:S(2)}) copy-start(bf16[512,2752]{0,1:T(8,128)(2,1)} %all-gather.5.cloned.1.call-done) | copy-start | bytes 8454148
Sparse Core Ops, SparseCore 0:
  9.5 13.7 all-gather.4
  27.2 63.2 reduce-scatter.5
  92.6 71.8 all-gather.2
  168.4 67.8 all-reduce.2
  238.4 13.1 reduce-scatter.3
where the time goes:
time: 268 us
  waiting for transfers between devices  198 us (74%)
  matrix products  42.3 us (16%)
  between operations  14.5 us (5%)
  blocking collectives  5.99 us (2%)
  other arithmetic  3.36 us (1%)
  local copies, waits for them, and re-layouts  3.16 us (1%)
    all_gather x1, waiting for transfers between devices, body(): full_grad = lax.all_gather(grad_out, 'row', axis=0, tiled=True)  71.5 us
    reduce_scatter x1, waiting for transfers between devices, body(): lax.psum_scatter(jnp.dot(token_rows, proj_in, preferred_element_type=jnp....  59.1 us
    psum x1, waiting for transfers between devices, body(): example_grads = lax.psum(partial_grads, 'row')  50.7 us
    dot_general x1, matrix products, body(): lax.dot_general(token_rows, down_weight, (((1,), (1,)), ((), ())), prefer...  19.1 us
    dot_general x1, matrix products, body(): lax.dot_general(full_hidden, full_grad, (((0,), (0,)), ((), ())), preferr...  17.6 us
    all_gather x1, waiting for transfers between devices, body(): full_hidden = lax.all_gather(hidden_act, 'col', axis=0, tiled=True)  15.3 us
  transfers between devices with their start and end apart: 5, of which 4 were waited for; matrix products, arithmetic and copies ran while one was open for 16% of the time, Pallas kernels for 0%

commit v1 on v0

--- a/solution.py
+++ b/solution.py
@@ -37,7 +37,7 @@
     labels = jnp.arange(EXAMPLES, dtype=jnp.int32)
     onehot = (example_ids[None, :] == labels[:, None]).astype(jnp.float32)
     partial_grads = jnp.dot(onehot, outer_terms, precision=lax.Precision.HIGHEST)
-    example_grads = lax.psum(partial_grads, "row")
+    example_grads = jnp.sum(lax.all_gather(partial_grads, "row"), axis=0)
     values = jnp.dot(queries.astype(jnp.float32), example_grads.T, precision=lax.Precision.HIGHEST)
     scores = lax.psum_scatter(values, "col", scatter_dimension=0, tiled=True)
     return (grad_hidden, weight_grad, scores)

time: 268 us -> 230 us (0.86)
  waiting for transfers between devices: 198 us -> 128 us
  blocking collectives: 5.99 us -> 37.4 us
    psum x1 -> x0, waiting for transfers between devices: 50.7 us -> none  [body(): example_grads = lax.psum(partial_grads, 'row')]
    all_gather x0 -> x1, blocking collectives: none -> 31.5 us  [body(): example_grads = jnp.sum(lax.all_gather(partial_grads, 'row'), axis=0)]
    reduce_scatter x1, waiting for transfers between devices: 59.1 us -> 39.8 us  [body(): lax.psum_scatter(jnp.dot(token_rows, proj_in, preferred_element_type=jnp....]
  transfers between devices with their start and end apart: 5 -> 4, of which waited for: 4 -> 3; matrix products, arithmetic and copies ran while one was open for 16% -> 20% of each run, Pallas kernels for 0% -> 0%
where the time goes in v1:
time: 230 us; the launch traced here: 229 us
  waiting for transfers between devices  128 us (56%)
  matrix products  42.2 us (18%)
  blocking collectives  37.4 us (16%)
  between operations  14.5 us (6%)
  other arithmetic  3.39 us (1%)
  local copies, waits for them, and re-layouts  3.14 us (1%)
    all_gather x1, waiting for transfers between devices, body(): full_grad = lax.all_gather(grad_out, 'row', axis=0, tiled=True)  72.6 us
    reduce_scatter x1, waiting for transfers between devices, body(): lax.psum_scatter(jnp.dot(token_rows, proj_in, preferred_element_type=jnp....  39.8 us
    all_gather x1, blocking collectives, body(): example_grads = jnp.sum(lax.all_gather(partial_grads, 'row'), axis=0)  31.5 us
    dot_general x1, matrix products, body(): lax.dot_general(token_rows, down_weight, (((1,), (1,)), ((), ())), prefer...  19.1 us
    dot_general x1, matrix products, body(): lax.dot_general(full_hidden, full_grad, (((0,), (0,)), ((), ())), preferr...  18.9 us
    all_gather x1, waiting for transfers between devices, body(): full_hidden = lax.all_gather(hidden_act, 'col', axis=0, tiled=True)  14.6 us
  transfers between devices with their start and end apart: 4, of which 3 were waited for; matrix products, arithmetic and copies ran while one was open for 20% of the time, Pallas kernels for 0%

profile of v1, /device:TPU:0, one launch (start us, length us, event | category | flops | bytes accessed | tf_op | source)
XLA Modules:
  0.0 229.2 jit_solution(10511493849910208291)
XLA Ops:
  7.2 0.0 copy-start
  7.2 0.0 all-gather.6.cloned.1.call-start
  7.2 0.7 all-gather.6.cloned.1.call-update
  7.9 0.0 all-gather.4.cloned.1.call-start
  8.0 0.7 all-gather.4.cloned.1.call-update
  8.7 0.0 reduce-scatter.6.cloned.1.call-start
  8.7 14.6 %all-gather.6.cloned.1.call-done = bf16[512,2752]{0,1:T(8,128)(2,1)} async-done(((bf16[256,2752]{0,1:T(8,128)(2,1)}), bf16[512,2752]{0,1:T(8,128)(2,1)}) %all-gather.6.cloned.1.call-update) | async-done | bytes 2818064 | tf_op jit(solution)/shard_map/all_gather | solution.py:10
  23.3 3.5 %fusion.3 = f32[512,64]{1,0:T(8,128)} fusion(bf16[512,2752]{0,1:T(8,128)(2,1)} %all-gather.6.cloned.1.call-done, bf16[2752,64]{0,1:T(8,128)(2,1)} %param.10), kind=kOutput, calls=%fused_computation.10 | convolution fusion | flops 180355072 | bytes 3301376 | tf_op jit(solution)/shard_map/dot_general | solution.py:26
  26.8 0.0 reduce-scatter.6.cloned.1.call-update
  26.8 0.0 reduce-scatter.4.cloned.1.call-start
  26.9 72.6 %all-gather.4.cloned.1.call-done = bf16[512,4096]{1,0:T(8,128)(2,1)} async-done(((bf16[64,4096]{1,0:T(8,128)(2,1)}), bf16[512,4096]{1,0:T(8,128)(2,1)}) %all-gather.4.cloned.1.call-update) | async-done | bytes 4194320 | tf_op jit(solution)/shard_map/all_gather | solution.py:11
  99.5 19.1 %fusion.2 = f32[512,2752]{0,1:T(8,128)} fusion(bf16[512,4096]{1,0:T(8,128)(2,1)} %all-gather.4.cloned.1.call-done, bf16[2752,4096]{1,0:T(8,128)(2,1)} %param.9), kind=kOutput, calls=%fused_computation.9 | convolution fusion | flops 11542724608 | bytes 32374784 | tf_op jit(solution)/shard_map/dot_general | solution.py:14
  118.6 0.0 copy-start.5
  118.6 0.0 copy-start.2
  118.6 0.0 copy-start.4
  118.6 0.0 reduce-scatter.4.cloned.1.call-update
  118.6 0.0 copy-start.3
  118.6 0.6 copy-done.5
  119.2 0.6 dynamic-slice
  120.4 0.0 copy-done
  120.5 0.0 copy-done.2
  120.5 0.3 fusion.4
  120.8 3.4 %psum.7 = f32[64,64]{1,0:T(8,128)S(1)} all-reduce(f32[64,64]{1,0:T(8,128)S(1)} %fusion.4), channel_id=1, replica_groups=mesh['grp'=2,'row'=8,'col'=2] {'col'}, use_global_device_ids=true, to_apply=%region_2.0 | all-reduce | flops 4096 | bytes 32768 | tf_op jit(solution)/shard_map/psum | solution.py:31
  124.2 39.8 %reduce-scatter.6.cloned.1.call-done = f32[64,64]{1,0:T(8,128)} async-done(((f32[512,64]{1,0:T(8,128)}), f32[64,64]{1,0:T(8,128)}) %reduce-scatter.6.cloned.1.call-update) | async-done | bytes 16400 | tf_op jit(solution)/shard_map/reduce_scatter | solution.py:25
  164.0 0.8 constant_dynamic-slice_fusion.1
  164.8 0.3 broadcast_multiply_fusion
  165.2 0.4 mul.24
  165.5 0.0 copy-done.4
  165.5 0.3 fusion
  165.8 31.5 %all-gather = f32[64,2048]{1,0:T(8,128)S(1)} all-gather(f32[8,2048]{1,0:T(8,128)S(1)} %fusion), channel_id=2, replica_groups=mesh['grp'=2,'row'=8,'col'=2] {'row'}, dimensions={0}, use_global_device_ids=true | all-gather | bytes 589824 | tf_op jit(solution)/shard_map/all_gather | solution.py:40
  197.4 0.0 copy-done.3
  197.4 0.1 convolution_bitcast_fusion
  197.5 2.5 %all-reduce = f32[16,8]{0,1:T(8,128)S(1)} all-reduce(f32[16,8]{0,1:T(8,128)S(1)} %convolution_bitcast_fusion), channel_id=5, replica_groups=mesh['grp'=2,'row'=8,'col'=2] {'col'}, use_global_device_ids=true, to_apply=%region_4.0.clone | all-reduce | flops 128 | bytes 1024
  200.0 0.1 constant_dynamic-slice_fusion
  200.1 0.7 copy.11
  200.8 0.0 copy-start.1
  200.8 18.9 %convolution_convert_fusion = bf16[2752,4096]{1,0:T(8,128)(2,1)} fusion(bf16[512,2752]{0,1:T(8,128)(2,1)} %all-gather.6.cloned.1.call-done, bf16[512,4096]{1,0:T(8,128)(2,1)} %all-gather.4.cloned.1.call-done), kind=kOutput, calls=%fused_computation | convolution fusion | flops 11553996800 | bytes 29556736 | tf_op jit(solution)/shard_map/dot_general | solution.py:21
  219.7 0.0 reduce-scatter.4.cloned.1.call-done
  219.7 3.0 %convert_element_type.8 = bf16[256,2752]{0,1:T(8,128)(2,1)} convert(f32[256,2752]{0,1:T(8,128)} %reduce-scatter.4.cloned.1.call-done) | non-fusion elementwise | flops 704512 | bytes 4227072 | tf_op jit(solution)/shard_map/convert_element_type | solution.py:20
  222.7 0.0 copy-done.1
  (1 shorter events, 0.0 us)
Async XLA Ops:
  7.2 113.3 %copy-start = (bf16[4096,64]{0,1:T(8,128)(2,1)S(1)}, bf16[4096,64]{0,1:T(8,128)(2,1)}, u32[]{:S(2)}) copy-start(bf16[4096,64]{0,1:T(8,128)(2,1)} %param.11) | copy-start | bytes 1572868
  7.2 16.1 %all-gather.6.cloned.1.call-start = ((), (), s32[]{:S(2)}) async-start(), calls=%async_computation.4 | async-start | bytes 4227072 | tf_op jit(solution)/shard_map/all_gather | solution.py:10
  7.9 91.5 %all-gather.4.cloned.1.call-start = ((), (), s32[]{:S(2)}) async-start(), calls=%async_computation.2 | async-start | bytes 4718592 | tf_op jit(solution)/shard_map/all_gather | solution.py:11
  8.7 155.3 %reduce-scatter.6.cloned.1.call-start = ((), (), s32[]{:S(2)}) async-start(), calls=%async_computation.5 | async-start | bytes 294912 | tf_op jit(solution)/shard_map/reduce_scatter | solution.py:25
  26.8 192.9 %reduce-scatter.4.cloned.1.call-start = ((), (), s32[]{:S(2)}) async-start(), calls=%async_computation.3 | async-start | bytes 8454144 | tf_op jit(solution)/shard_map/reduce_scatter | solution.py:13
  118.6 0.7 copy-start.5
  118.6 1.9 copy-start.2
  118.6 47.0 %copy-start.4 = (s32[64]{0:T(128)S(1)}, s32[64]{0:T(128)}, u32[]{:S(2)}) copy-start(s32[64]{0:T(128)} %param.13) | copy-start | bytes 772
  118.6 78.8 %copy-start.3 = (bf16[16,2048]{1,0:T(8,128)(2,1)S(1)}, bf16[16,2048]{1,0:T(8,128)(2,1)}, u32[]{:S(2)}) copy-start(bf16[16,2048]{1,0:T(8,128)(2,1)} %param.12) | copy-start | bytes 196612
  200.8 21.9 %copy-start.1 = (bf16[4096,64]{0,1:T(8,128)(2,1)S(1)}, bf16[4096,64]{0,1:T(8,128)(2,1)}, u32[]{:S(2)}) copy-start(bf16[4096,64]{0,1:T(8,128)(2,1)} %param.11) | copy-start | bytes 1572868
Sparse Core Ops, SparseCore 0:
  9.5 13.7 all-gather.5
  25.4 73.9 all-gather.3
  103.4 60.5 reduce-scatter.5
  166.1 12.2 reduce-scatter.3
